TPU v7x, 32 devices: a whole 2x2x4 slice. The times are simulated.
32 devices in a mesh: chan: 16 (over z, x, core), pix: 2 (over y).
Axes of the slice: x: 2, y: 2, z: 4, core: 2. Of those that a mesh axis runs over, the one named last changes fastest.
Arguments:
- cube: float32 [512, 16384], P('pix', 'chan'), as said below
- windows: int32 [8], replicated, may hold values from 1 to 1024, as said below
- mask: int32 [16384], replicated, may hold values from 0 to 1, as said below
Outputs:
- subtracted: float32 [512, 16384], P('pix', 'chan')
Inputs may be any that keep to these rules, and one draw needn't show every extreme that they name: windows[0] is 1024 and windows[7] is 1; for 0 < k < 7, windows[k] is at most 1024 halved k times (rounded down) and more than three quarters of that, but 1 or more. `mask`: zero on 8 disjoint ranges of 256 to 512 channels each, one elsewhere; the k-th range lies inside channels k * 2048 to (k + 1) * 2048 - 1, at least 512 channels from that slot's edges, and at least 1024 channels from either end of the band. `cube`: each spectrum is a smooth continuum of low order plus noise whose level varies from channel to channel.
All inputs are finite; a program needn't handle non-finite values.
Results may differ from a plain program's by a relative error of at most 0.00021.
Values sent between devices are 32-bit elements; how exact they have to be, the bound alone decides.
A program may use at most 64 MiB of HBM per device.

v0:
```python
import jax
import jax.numpy as jnp
from jax import lax
from jax.sharding import PartitionSpec as P

TERMS = 16
PASSES = 8
WMAX = 1024


def legendre(xvals):
    rows = [jnp.ones_like(xvals), xvals]
    for order in range(1, TERMS - 1):
        rows.append(
            ((2.0 * order + 1.0) * xvals * rows[order] - order * rows[order - 1]) / (order + 1.0)
        )
    return jnp.stack(rows[:TERMS], axis=0)


def channel_x(start, count, total):
    index = start + lax.broadcasted_iota(jnp.int32, (count,), 0)
    return (2.0 * index.astype(jnp.float32) + 1.0) / total - 1.0


def snip(spectra, windows):
    count = spectra.shape[1]
    column = lax.broadcasted_iota(jnp.int32, (1, count), 1)
    for step in range(PASSES):
        width = windows[step]
        padded = jnp.pad(spectra, ((0, 0), (WMAX, WMAX)))
        lower = lax.dynamic_slice_in_dim(padded, WMAX - width, count, 1)
        upper = lax.dynamic_slice_in_dim(padded, WMAX + width, count, 1)
        inside = (column >= width) & (column < count - width)
        spectra = jnp.where(inside, jnp.minimum(spectra, 0.5 * (lower + upper)), spectra)
    return spectra


def per_device(cube, windows, mask):
    ch_dev = cube.shape[1]
    n_chan = lax.axis_size("chan")
    total = ch_dev * n_chan
    pix_rows = cube.shape[0] // n_chan
    table = legendre(channel_x(0, total, total))
    weighted = table * mask.astype(jnp.float32)[None, :]
    gram = jnp.dot(weighted, table.T, precision=lax.Precision.HIGHEST)
    factor = jnp.linalg.cholesky(gram)
    blocks = cube.reshape(n_chan, pix_rows, ch_dev)
    baseline = snip(
        lax.all_to_all(blocks, "chan", split_axis=0, concat_axis=2, tiled=True)[0], windows
    )
    rhs = jnp.dot(weighted, baseline.T, precision=lax.Precision.HIGHEST)
    middle = lax.linalg.triangular_solve(factor, rhs, left_side=True, lower=True)
    result = lax.linalg.triangular_solve(
        factor, middle, left_side=True, lower=True, transpose_a=True
    ).T[None]
    coef_all = lax.all_gather(result[0], "chan", axis=0, tiled=True)
    start = lax.axis_index("chan") * ch_dev
    local_table = legendre(channel_x(start, ch_dev, total))
    return cube - jnp.dot(coef_all, local_table, precision=lax.Precision.HIGHEST)


def solution(mesh):
    placed = (P("pix", "chan"), P(), P())
    return jax.shard_map(
        per_device, mesh=mesh, in_specs=placed, out_specs=P("pix", "chan"), check_vma=False
    )
```

profile of v0, /device:TPU:0, one launch (start us, length us, event | category | flops | bytes accessed | tf_op | source)
XLA Modules:
  0.0 83.6 jit_solution(13126200222864727361)
XLA Ops:
  0.0 7.5 %all-to-all-start = ((f32[16,16,1024]{2,1,0:T(8,128)}), f32[16,16,1024]{2,1,0:T(8,128)S(1)}, u32[]{:S(2)}, u32[]{:S(2)}) async-start(f32[16,16,1024]{2,1,0:T(8,128)} %bitcast.33), calls=%async_computation | async-start | bytes 2097152 | tf_op jit(solution)/shard_map/all_to_all | solution.py:49
  7.5 0.7 fusion.43
  33.3 1.3 %subtract_multiply_fusion = (f32[1,16384]{1,0:T(1,128)S(1)}, f32[1,16384]{1,0:T(1,128)S(1)}) fusion(), kind=kLoop, calls=%fused_computation.67 | loop fusion | flops 1212416 | bytes 131072 | tf_op jit(solution)/shard_map/div | solution.py:15
  34.6 1.1 %multiply_add_fusion = (f32[1,16384]{1,0:T(1,128)S(1)}, f32[1,16384]{1,0:T(1,128)S(1)}) fusion(), kind=kLoop, calls=%fused_computation.80 | loop fusion | flops 1048576 | bytes 131072 | tf_op jit(solution)/shard_map/sub | solution.py:22
  35.7 1.0 %broadcast_multiply_fusion.1 = (f32[1,16384]{1,0:T(1,128)S(1)}, f32[1,16384]{1,0:T(1,128)S(1)}) fusion(), kind=kLoop, calls=%fused_computation.90 | loop fusion | flops 966656 | bytes 131072 | tf_op jit(solution)/shard_map/div | solution.py:15
  36.7 0.9 %broadcast_multiply_fusion.3 = (f32[1,16384]{1,0:T(1,128)S(1)}, f32[1,16384]{1,0:T(1,128)S(1)}) fusion(), kind=kLoop, calls=%fused_computation.92 | loop fusion | flops 802816 | bytes 131072 | tf_op jit(solution)/shard_map/div | solution.py:15
  37.6 0.7 broadcast_multiply_fusion.5
  40.0 1.8 %stack.4 = f32[16,16384]{1,0:T(8,128)S(1)} concatenate(f32[1,16384]{1,0:T(1,128)S(1)} %stack_broadcast_in_dim.6, f32[1,16384]{1,0:T(1,128)S(1)} %get-tuple-element.15, f32[1,16384]{1,0:T(1,128)S(1)} %broadcast_multiply_fusion.11, f32[1,16384]{1,0:T(1,128)S(1)} %get-tuple-element.26, f32[1,16384]{1,0:T(1,128)S(1)} %get-tuple-element.25, f32[1,16384]{1,0:T(1,128)S(1)} %get-tuple-element.24, ...), dimensions={0} | concatenate | bytes 2097152 | tf_op jit(solution)/shard_map/stack | solution.py:17
  41.8 1.5 %fusion.2 = f32[16,16]{1,0:T(8,128)S(1)} fusion(f32[16,16384]{1,0:T(8,128)S(1)} %stack.4, f32[16384]{0:T(1024)S(1)} %convert_element_type.173), kind=kOutput, calls=%fused_computation.10 | convolution fusion | flops 50593792 | bytes 1115136 | tf_op jit(solution)/shard_map/dot_general | solution.py:45
  43.4 1.5 %cholesky.16 = f32[16,16]{1,0:T(8,128)S(1)} custom-call(f32[16,16]{1,0:T(8,128)S(1)} %fusion.38), custom_call_target="Cholesky" | custom-call | tf_op jit(solution)/shard_map/jit(cholesky)/cholesky | solution.py:46
  44.9 0.7 compare_reduce_fusion
  46.2 1.2 %custom-call.8 = f32[1,16,16]{1,2,0:T(8,128)S(1)} custom-call(f32[1,16,16]{2,1,0:T(8,128)S(1)} %fusion.33), custom_call_target="InvertDiagBlocksLowerTriangular" | custom-call | tf_op jit(solution)/shard_map/triangular_solve | solution.py:53
  47.6 0.7 fusion.32
  48.9 0.6 fusion.30
  49.6 0.6 fusion.29
  50.2 0.7 fusion.28
  51.4 0.7 fusion.26
  52.1 0.7 fusion.25
  53.6 0.6 minimum_select_fusion.6
  54.2 0.6 minimum_select_fusion.5
  54.9 0.6 minimum_select_fusion.4
  57.4 1.7 %fusion = f32[16,16]{1,0:T(8,128)S(1)} fusion(f32[16,16384]{1,0:T(8,128)S(1)} %stack.4, f32[16,16384]{1,0:T(8,128)S(1)} %minimum_select_fusion.1, s32[]{:T(128)S(6)} %select_n.99, s32[]{:T(128)S(6)} %select_n.100, f32[16384]{0:T(1024)S(1)} %convert_element_type.173, pred[16384]{0:T(1024)(128)(4,1)S(1)} %fusion.25), kind=kOutput, calls=%fused_computation.8 | convolution fusion | flops 51642368 | bytes 2180104 | tf_op jit(solution)/shard_map/dot_general | solution.py:51
  59.6 22.1 %all_gather.3 = f32[256,16]{1,0:T(8,128)S(1)} all-gather(f32[16,16]{1,0:T(8,128)S(1)} %fusion.34), channel_id=1, replica_groups=mesh['chan'=16,'pix'=2] {'chan'}, dimensions={0}, use_global_device_ids=true | all-gather | bytes 17408 | tf_op jit(solution)/shard_map/all_gather | solution.py:56
  81.6 2.0 %convolution_subtract_fusion = f32[256,1024]{1,0:T(8,128)} fusion(f32[256,1024]{1,0:T(8,128)S(1)} %copy-done, f32[256,16]{1,0:T(8,128)S(1)} %all_gather.3, f32[16,1024]{1,0:T(8,128)S(1)} %stack.5), kind=kOutput, calls=%fused_computation.12 | convolution fusion | flops 50593792 | bytes 2179072 | tf_op jit(solution)/shard_map/dot_general | solution.py:59
  (35 shorter events, 6.7 us)
Async XLA Ops:
  0.0 7.5 %copy-start.2 = (s32[8]{0:T(128)S(1)}, s32[8]{0:T(128)}, u32[]{:S(2)}) copy-start(s32[8]{0:T(128)} %param.4) | copy-start | bytes 100
  0.0 52.8 %all-to-all-start = ((f32[16,16,1024]{2,1,0:T(8,128)}), f32[16,16,1024]{2,1,0:T(8,128)S(1)}, u32[]{:S(2)}, u32[]{:S(2)}) async-start(f32[16,16,1024]{2,1,0:T(8,128)} %bitcast.33), calls=%async_computation | async-start | bytes 2097152 | tf_op jit(solution)/shard_map/all_to_all | solution.py:49
  7.5 32.4 %copy-start.1 = (s32[16384]{0:T(1024)S(1)}, s32[16384]{0:T(1024)}, u32[]{:S(2)}) copy-start(s32[16384]{0:T(1024)} %param.5) | copy-start | bytes 196612
  57.4 24.2 %copy-start = (f32[256,1024]{1,0:T(8,128)S(1)}, f32[256,1024]{1,0:T(8,128)}, u32[]{:S(2)}) copy-start(f32[256,1024]{1,0:T(8,128)} %param.3) | copy-start | bytes 3145732
where the time goes:
time: 84.2 us; the launch traced here: 83.6 us
  between operations  25.4 us (30%)
  blocking collectives  22.1 us (26%)
  other arithmetic  20.2 us (24%)
  starting transfers between devices  7.52 us (9%)
  matrix products  5.55 us (7%)
  local copies, waits for them, and re-layouts  2.86 us (3%)
    all_gather x1, blocking collectives, per_device(): coef_all = lax.all_gather(result[0], 'chan', axis=0, tiled=True)  22.1 us
    all_to_all x1, starting transfers between devices, per_device(): lax.all_to_all(blocks, 'chan', split_axis=0, concat_axis=2, tiled=True)[0]  7.52 us
    div x14, other arithmetic, legendre(): ((2.0 * order + 1.0) * xvals * rows[order] - order * rows[order - 1]) / (...  5.35 us
    and x8, other arithmetic, snip(): inside = (column >= width) & (column < count - width)  5.17 us
    select_n x7, other arithmetic, snip(): jnp.where(inside, jnp.minimum(spectra, 0.5 * (lower + upper)), spectra)  4.44 us
    another operation x3, other arithmetic, per_device(): factor = jnp.linalg.cholesky(gram)  2.16 us
    another operation x4, local copies, waits for them, and re-layouts, legendre(): return jnp.stack(rows[:TERMS], axis=0)  2 us
    dot_general x1, matrix products, per_device(): jnp.dot(coef_all, local_table, precision=lax.Precision.HIGHEST)  1.96 us
  transfers between devices with their start and end apart: 1, of which 0 were waited for; matrix products, arithmetic and copies ran while one was open for 24% of the time, Pallas kernels for 0%

commit v1 on v0

v1 whole, which is shorter than its diff:
```python
import functools
import math

import jax
import jax.numpy as jnp
import numpy as np
from jax import lax
from jax.experimental import pallas as pl
from jax.experimental.pallas import tpu as pltpu
from jax.sharding import PartitionSpec as P

TERMS = 16
PASSES = 8
WMAX = 1024
HALO = 2 * WMAX
LANES = 128
BLOCK = 16
CHUNKS = 4
MESH = pl.DeviceIdType.MESH
F32 = jnp.float32
BF16 = jnp.bfloat16


def linearization():
    def a(r):
        return math.comb(2 * r, r) / 2.0**r

    out = np.zeros((2 * TERMS - 1, TERMS, TERMS))
    for n in range(TERMS):
        for m in range(TERMS):
            for r in range(min(n, m) + 1):
                k = n + m - 2 * r
                out[k, n, m] = (
                    a(r) * a(n - r) * a(m - r) / a(n + m - r)
                    * (2 * k + 1) / (2 * n + 2 * m - 2 * r + 1)
                )
    return out.astype(np.float32)


def next_legendre(order, xvals, here, before):
    return ((2.0 * order + 1.0) * xvals * here - order * before) * (1.0 / (order + 1.0))


def split3(v):
    hi = v.astype(BF16)
    rest = v - hi.astype(F32)
    mid = rest.astype(BF16)
    lo = (rest - mid.astype(F32)).astype(BF16)
    return hi, mid, lo


def kernel(
    n_chan, group, total,
    windows, cube, mask_sq, mask_row, lin,
    out,
    held, raw, ping, pong, fit_hi, fit_lo, table, w3, sums,
    load_sem, own_sem, send_sem, hop_sem, recv_sem, up_sem, down_sem, sum_send, sum_recv,
):
    pix, ch = held.shape
    rows = raw.shape[0]
    slab_ch = group * ch
    tiles = slab_ch // LANES
    slabs = n_chan // group
    part = rows // CHUNKS
    me = lax.axis_index("chan")
    slab = me // group
    g = lax.rem(me, group)
    own_col = pl.multiple_of(HALO + g * ch, LANES)

    def peer(b):
        return {"chan": slab * group + b}

    load = pltpu.make_async_copy(cube, held, load_sem)
    load.start()
    barrier = pltpu.get_barrier_semaphore()
    for k in range(1, n_chan):
        pl.semaphore_signal(
            barrier, inc=1, device_id={"chan": lax.rem(me + k, n_chan)}, device_id_type=MESH
        )

    @pl.when(slab == 0)
    def _():
        raw[:, 0:HALO] = jnp.full((rows, HALO), jnp.inf, F32)

    @pl.when(slab == slabs - 1)
    def _():
        raw[:, HALO + slab_ch :] = jnp.full((rows, HALO), jnp.inf, F32)

    load.wait()
    own_rows = pl.multiple_of(g * rows, 8)
    own = pltpu.make_async_copy(
        held.at[pl.ds(own_rows, rows), :], raw.at[:, pl.ds(own_col, ch)], own_sem
    )
    own.start()
    pl.semaphore_wait(barrier, n_chan - 1)

    def chunk(c):
        return pl.ds(c * part, part)

    def slab_send(c, b):
        return pltpu.make_async_remote_copy(
            src_ref=held.at[pl.ds(b * rows + c * part, part), :],
            dst_ref=raw.at[chunk(c), pl.ds(own_col, ch)],
            send_sem=send_sem, recv_sem=recv_sem.at[c, g],
            device_id=peer(b), device_id_type=MESH,
        )

    def slab_recv(c, b):
        return pltpu.make_async_remote_copy(
            src_ref=held.at[pl.ds(c * part, part), :],
            dst_ref=raw.at[chunk(c), pl.ds(HALO + b * ch, ch)],
            send_sem=send_sem, recv_sem=recv_sem.at[c, b],
            device_id=peer(b), device_id_type=MESH,
        )

    def hop(c, b, up, from_own):
        if up:
            col = b * ch - (slab_ch - HALO)
            sem, to = up_sem.at[c], me + group
        else:
            col = HALO + slab_ch + b * ch
            sem, to = down_sem.at[c], me - group
        if from_own:
            src = held.at[pl.ds(pl.multiple_of(own_rows + c * part, 8), part), :]
        else:
            src = raw.at[chunk(c), pl.ds(HALO + b * ch, ch)]
        return pltpu.make_async_remote_copy(
            src_ref=src, dst_ref=raw.at[chunk(c), pl.ds(col, ch)],
            send_sem=hop_sem.at[0 if up else 1], recv_sem=sem,
            device_id={"chan": to}, device_id_type=MESH,
        )

    def goes_up(b):
        return b * ch >= slab_ch - HALO

    def goes_down(b):
        return b * ch < HALO

    def own_hops(c):
        for b in range(group):
            if goes_up(b):
                @pl.when((g == b) & (slab < slabs - 1))
                def _():
                    hop(c, b, True, True).start()
            if goes_down(b):
                @pl.when((g == b) & (slab > 0))
                def _():
                    hop(c, b, False, True).start()

    def forward(c):
        for b in range(group):
            @pl.when(g != b)
            def _():
                slab_recv(c, b).wait_recv()
                if goes_up(b):
                    @pl.when(slab < slabs - 1)
                    def _():
                        hop(c, b, True, False).start()
                if goes_down(b):
                    @pl.when(slab > 0)
                    def _():
                        hop(c, b, False, False).start()

    def halo_wait(c):
        def arrived(col, sem):
            return pltpu.make_async_remote_copy(
                src_ref=raw.at[chunk(c), pl.ds(col, HALO)],
                dst_ref=raw.at[chunk(c), pl.ds(col, HALO)],
                send_sem=hop_sem.at[0], recv_sem=sem,
                device_id={"chan": me}, device_id_type=MESH,
            )

        @pl.when(slab > 0)
        def _():
            arrived(0, up_sem.at[c]).wait_recv()

        @pl.when(slab < slabs - 1)
        def _():
            arrived(HALO + slab_ch, down_sem.at[c]).wait_recv()

    for c in range(CHUNKS):
        for b in range(group):
            @pl.when(g != b)
            def _():
                slab_send(c, b).start()
        own_hops(c)

    shape = mask_sq.shape
    index = lax.broadcasted_iota(jnp.int32, shape, 0) * shape[1] + lax.broadcasted_iota(
        jnp.int32, shape, 1
    )
    xvals = (2.0 * index.astype(F32) + 1.0) * (1.0 / total) - 1.0
    keep = mask_sq[...].astype(F32)
    here, before = jnp.ones_like(xvals), jnp.zeros_like(xvals)
    gram = jnp.zeros((TERMS, TERMS), F32)
    for k in range(2 * TERMS - 1):
        moment = jnp.sum(here * keep, axis=0, keepdims=True)
        moment = jnp.sum(moment, axis=1, keepdims=True)
        gram = gram + moment * lin[k]
        here, before = next_legendre(k, xvals, here, before), here

    row_id = lax.broadcasted_iota(jnp.int32, (TERMS, 2 * TERMS), 0)
    col_id = lax.broadcasted_iota(jnp.int32, (TERMS, 2 * TERMS), 1)
    eye = jnp.where(row_id + TERMS == col_id, 1.0, 0.0).astype(F32)
    aug = eye + jnp.concatenate([gram, jnp.zeros_like(gram)], axis=1)
    for p in range(TERMS):
        lead = aug[p : p + 1, :] / aug[p : p + 1, p : p + 1]
        aug = jnp.where(row_id == p, lead, aug - aug[:, p : p + 1] * lead)
    inverse = aug[:, TERMS:]

    forward(0)

    step = min(1024, slab_ch)
    base = slab * slab_ch
    for s in range(0, slab_ch, step):
        lane = lax.broadcasted_iota(jnp.int32, (1, step), 1)
        x_s = (2.0 * (base + s + lane).astype(F32) + 1.0) * (1.0 / total) - 1.0
        here, before = jnp.ones_like(x_s), jnp.zeros_like(x_s)
        for n in range(TERMS):
            table[n : n + 1, s : s + step] = here
            here, before = next_legendre(n, x_s, here, before), here
        keep_s = mask_row[:, pl.ds(pl.multiple_of(base + s, LANES), step)].astype(F32)
        hi, mid, lo = split3(table[:, s : s + step] * keep_s)
        w3[0:TERMS, s : s + step] = hi
        w3[TERMS : 2 * TERMS, s : s + step] = mid
        w3[2 * TERMS :, s : s + step] = lo

    forward(1)

    own.wait()
    lane = lax.broadcasted_iota(jnp.int32, (BLOCK, LANES), 1)
    edge = HALO // LANES

    def snip(start):
        r = pl.ds(start, BLOCK)

        def at(ref, t):
            return ref[:, (t + edge) * LANES : (t + edge + 1) * LANES]

        def put(ref, t, v):
            ref[:, (t + edge) * LANES : (t + edge + 1) * LANES] = v

        def first(t):
            return raw[r, (t + edge) * LANES : (t + edge + 1) * LANES]

        far = WMAX // LANES
        for t in range(-far, tiles + far):
            put(ping, t, jnp.minimum(first(t), 0.5 * (first(t - far) + first(t + far))))
        src, dst = ping, pong
        for k in range(1, PASSES):
            bound = max(LANES, WMAX >> k)
            b = bound // LANES
            d = bound - windows[k]
            back = lax.rem(LANES - d, LANES)
            low_here = lane < LANES - d
            high_here = lane >= d
            reach = 0 if k == PASSES - 1 else b
            left = {}
            right = {}
            for t in range(-reach, tiles + reach):
                for u in (t - b, t - b + 1):
                    if u not in left:
                        left[u] = pltpu.roll(at(src, u), back, 1)
                for u in (t + b - 1, t + b):
                    if u not in right:
                        right[u] = pltpu.roll(at(src, u), d, 1)
                lower = jnp.where(low_here, left[t - b], left[t - b + 1])
                upper = jnp.where(high_here, right[t + b], right[t + b - 1])
                v = jnp.minimum(at(src, t), 0.5 * (lower + upper))
                if k < PASSES - 1:
                    put(dst, t, v)
                else:
                    cols = slice(t * LANES, (t + 1) * LANES)
                    hi = v.astype(BF16)
                    fit_hi[r, cols] = hi
                    fit_lo[r, cols] = (v - hi.astype(F32)).astype(BF16)
            src, dst = dst, src

    def process(c):
        halo_wait(c)
        blocks = part // BLOCK
        if blocks == 1:
            snip(c * part)
        else:
            def body(i, carry):
                snip(pl.multiple_of(c * part + i * BLOCK, BLOCK))
                return carry
            lax.fori_loop(0, blocks, body, 0)

    for c in range(CHUNKS):
        if c + 2 < CHUNKS:
            forward(c + 2)
        process(c)

    dims = (((1,), (1,)), ((), ()))
    rhs3 = lax.dot_general(w3[...], fit_hi[...], dims, preferred_element_type=F32)
    rhs3 = rhs3 + lax.dot_general(w3[...], fit_lo[...], dims, preferred_element_type=F32)
    rhs = rhs3[0:TERMS] + (rhs3[TERMS : 2 * TERMS] + rhs3[2 * TERMS :])
    fold = sums.shape[2] // rows
    high = TERMS // fold
    packed = jnp.concatenate([rhs[i * high : (i + 1) * high] for i in range(fold)], axis=1)
    sums[me] = packed

    def sum_copy(k):
        return pltpu.make_async_remote_copy(
            src_ref=sums.at[me], dst_ref=sums.at[me],
            send_sem=sum_send, recv_sem=sum_recv,
            device_id={"chan": lax.rem(me + k, n_chan)}, device_id_type=MESH,
        )

    for k in range(1, n_chan):
        sum_copy(k).start()

    t_own = table[:, pl.ds(pl.multiple_of(g * ch, LANES), ch)]
    shaped = jnp.zeros_like(t_own)
    for m in range(TERMS):
        shaped = shaped + inverse[:, m : m + 1] * t_own[m : m + 1, :]
    a_hi, a_mid, a_lo = split3(shaped)
    zero = jnp.zeros_like(a_hi)
    right_side = jnp.concatenate([a_hi, a_mid, a_hi, a_lo, a_hi, a_mid, zero, zero], axis=0)

    def sent(ref, sem):
        return pltpu.make_async_remote_copy(
            src_ref=ref, dst_ref=ref, send_sem=sem, recv_sem=own_sem,
            device_id={"chan": me}, device_id_type=MESH,
        )

    if group > 1:
        sent(held.at[0 : (group - 1) * rows, :], send_sem).wait_send()

    @pl.when(slab < slabs - 1)
    def _():
        sent(raw.at[:, 0:HALO], hop_sem.at[0]).wait_send()

    @pl.when(slab > 0)
    def _():
        sent(raw.at[:, 0:HALO], hop_sem.at[1]).wait_send()

    others = sums.at[0 : n_chan - 1]
    everyone = pltpu.make_async_remote_copy(
        src_ref=others, dst_ref=others, send_sem=sum_send, recv_sem=sum_recv,
        device_id={"chan": me}, device_id_type=MESH,
    )
    everyone.wait_send()
    everyone.wait_recv()

    for b in range(group):
        tot = sums[b]
        for z in range(1, slabs):
            tot = tot + sums[z * group + b]
        tot = jnp.concatenate(
            [tot[:, i * rows : (i + 1) * rows] for i in range(fold)], axis=0
        )
        hi, mid, lo = (v.astype(F32) for v in split3(tot))
        none = jnp.zeros_like(hi)
        left_side = jnp.concatenate([hi, hi, mid, hi, lo, mid, none, none], axis=0)
        left_side = left_side.T.astype(BF16)
        r = slice(b * rows, (b + 1) * rows)
        out[r, :] = held[r, :] - jnp.dot(left_side, right_side, preferred_element_type=F32)


def per_device(cube, windows, mask):
    pix, ch = cube.shape
    n_chan = lax.axis_size("chan")
    total = ch * n_chan
    group = min(n_chan, max(4, HALO // ch))
    slab_ch = group * ch
    rows = pix // group
    wide = slab_ch + 2 * HALO
    fold = max(1, LANES // rows)
    vmem = pl.BlockSpec(memory_space=pltpu.VMEM)
    dma = pltpu.SemaphoreType.DMA
    return pl.pallas_call(
        functools.partial(kernel, n_chan, group, total),
        out_shape=jax.ShapeDtypeStruct((pix, ch), F32),
        in_specs=[
            pl.BlockSpec(memory_space=pltpu.SMEM),
            pl.BlockSpec(memory_space=pl.ANY),
            vmem, vmem, vmem,
        ],
        out_specs=vmem,
        scratch_shapes=[
            pltpu.VMEM((pix, ch), F32),
            pltpu.VMEM((rows, wide), F32),
            pltpu.VMEM((BLOCK, wide), F32),
            pltpu.VMEM((BLOCK, wide), F32),
            pltpu.VMEM((rows, slab_ch), BF16),
            pltpu.VMEM((rows, slab_ch), BF16),
            pltpu.VMEM((TERMS, slab_ch), F32),
            pltpu.VMEM((3 * TERMS, slab_ch), BF16),
            pltpu.VMEM((n_chan, TERMS // fold, rows * fold), F32),
            dma, dma, dma, dma((2,)),
            dma((CHUNKS, group)), dma((CHUNKS,)), dma((CHUNKS,)),
            dma, dma,
        ],
        compiler_params=pltpu.CompilerParams(collective_id=0, has_side_effects=True),
    )(
        windows, cube, mask.reshape(-1, LANES), mask.reshape(1, total),
        jnp.asarray(linearization()),
    )


def solution(mesh):
    placed = (P("pix", "chan"), P(), P())
    return jax.shard_map(
        per_device, mesh=mesh, in_specs=placed, out_specs=P("pix", "chan"), check_vma=False
    )
```

time: 84.2 us -> 33.1 us (0.39)
  Pallas kernels: 0 us -> 30.6 us
  between operations: 25.4 us -> 0.01 us
  blocking collectives: 22.1 us -> 0 us
  other arithmetic: 20.2 us -> 0 us
  starting transfers between devices: 7.52 us -> 0 us
  matrix products: 5.55 us -> 0 us
    pallas_call x0 -> x1, Pallas kernels: none -> 30.6 us  [per_device(): pl.pallas_call(functools.partial(kernel, n_chan, group, total), out_shape...]
    all_gather x1 -> x0, blocking collectives: 22.1 us -> none  [per_device(): coef_all = lax.all_gather(result[0], 'chan', axis=0, tiled=True)]
    all_to_all x1 -> x0, starting transfers between devices: 7.52 us -> none  [per_device(): lax.all_to_all(blocks, 'chan', split_axis=0, concat_axis=2, tiled=True)[0]]
    div x15 -> x0, other arithmetic: 5.36 us -> none  [the longest x14 5.35 us: legendre(): ((2.0 * order + 1.0) * xvals * rows[order] - order * rows[order - 1]) / (...]
    and x8 -> x0, other arithmetic: 5.17 us -> none  [snip(): inside = (column >= width) & (column < count - width)]
    dot_general x3 -> x0, matrix products: 5.13 us -> none  [the longest x1 1.96 us: per_device(): jnp.dot(coef_all, local_table, precision=lax.Precision.HIGHEST)]
    select_n x7 -> x0, other arithmetic: 4.44 us -> none  [snip(): jnp.where(inside, jnp.minimum(spectra, 0.5 * (lower + upper)), spectra)]
    another operation x5 -> x0, other arithmetic: 4.01 us -> none  [the longest x3 2.16 us: per_device(): factor = jnp.linalg.cholesky(gram)]
  transfers between devices with their start and end apart: 1 -> 0, of which waited for: 0 -> 0; matrix products, arithmetic and copies ran while one was open for 24% -> 0% of each run, Pallas kernels for 0% -> 0%
where the time goes in v1:
time: 33.1 us; the launch traced here: 32.9 us
  Pallas kernels  30.6 us (92%)
  local copies, waits for them, and re-layouts  2.31 us (7%)
    pallas_call x1, Pallas kernels, per_device(): pl.pallas_call(functools.partial(kernel, n_chan, group, total), out_shape...  30.6 us
    unnamed x1, local copies, waits for them, and re-layouts  2.31 us

profile of v1, /device:TPU:0, one launch (start us, length us, event | category | flops | bytes accessed | tf_op | source)
XLA Modules:
  0.0 32.9 jit_solution(2667290318050585233)
XLA Ops:
  0.0 30.6 %shard_map.46 = f32[256,1024]{1,0:T(8,128)} custom-call(s32[8]{0:T(128)} %windows.1, f32[256,1024]{1,0:T(8,128)} %cube.1, s32[128,128]{1,0:T(8,128)} %bitcast.2, s32[1,16384]{1,0:T(1,128)} %bitcast.3, f32[31,16,16]{2,1,0:T(8,128)} %constant.2.clone.lin), custom_call_target="tpu_custom_call" | custom-call | tf_op jit(solution)/shard_map/pallas_call | solution.py:373
  30.6 2.3 %copy.6 = f32[256,1024]{1,0:T(8,128)} copy(f32[256,1024]{1,0:T(8,128)} %shard_map.46) | data formatting | bytes 2097152

commit v2 on v1

--- a/solution.py
+++ b/solution.py
@@ -16,9 +16,20 @@
 LANES = 128
 BLOCK = 16
 CHUNKS = 4
+SPLIT = 2
+TAIL = True
 MESH = pl.DeviceIdType.MESH
 F32 = jnp.float32
 BF16 = jnp.bfloat16
+
+
+def chunk_spans(rows):
+    part = rows // CHUNKS
+    sizes = [part] * CHUNKS
+    if TAIL and part >= 16:
+        sizes[-1:] = [part // 2, part // 2]
+    starts = [sum(sizes[:i]) for i in range(len(sizes))]
+    return list(zip(starts, sizes))
 
 
 def linearization():
@@ -51,17 +62,17 @@
 
 def kernel(
     n_chan, group, total,
-    windows, cube, mask_sq, mask_row, lin,
-    out,
-    held, raw, ping, pong, fit_hi, fit_lo, table, w3, sums,
-    load_sem, own_sem, send_sem, hop_sem, recv_sem, up_sem, down_sem, sum_send, sum_recv,
+    windows, cube, mask_sq_hbm, mask_row_hbm, lin_hbm,
+    left_out, right_out,
+    mask_sq, mask_row, lin, raw, ping, pong, fit, table, w3, sums,
+    load_sem, token, own_sem, send_sem, hop_sem, recv_sem, up_sem, down_sem, sum_send, sum_recv,
 ):
-    pix, ch = held.shape
+    pix, ch = cube.shape
     rows = raw.shape[0]
     slab_ch = group * ch
     tiles = slab_ch // LANES
     slabs = n_chan // group
-    part = rows // CHUNKS
+    spans = chunk_spans(rows)
     me = lax.axis_index("chan")
     slab = me // group
     g = lax.rem(me, group)
@@ -70,13 +81,36 @@
     def peer(b):
         return {"chan": slab * group + b}
 
-    load = pltpu.make_async_copy(cube, held, load_sem)
-    load.start()
+    own_rows = pl.multiple_of(g * rows, 8)
     barrier = pltpu.get_barrier_semaphore()
-    for k in range(1, n_chan):
+
+    def greet(device):
         pl.semaphore_signal(
-            barrier, inc=1, device_id={"chan": lax.rem(me + k, n_chan)}, device_id_type=MESH
-        )
+            barrier, inc=1, device_id={"chan": device}, device_id_type=MESH
+        )
+
+    for k in range(1, group):
+        greet(slab * group + lax.rem(g + k, group))
+
+    @pl.when(slab > 0)
+    def _():
+        greet(me - group)
+
+    @pl.when(slab < slabs - 1)
+    def _():
+        greet(me + group)
+
+    loads = [
+        pltpu.make_async_copy(mask_sq_hbm, mask_sq, load_sem.at[0]),
+        pltpu.make_async_copy(mask_row_hbm, mask_row, load_sem.at[1]),
+        pltpu.make_async_copy(lin_hbm, lin, load_sem.at[2]),
+    ]
+    own = pltpu.make_async_copy(
+        cube.at[pl.ds(own_rows, rows), :], raw.at[:, pl.ds(own_col, ch)], own_sem
+    )
+    for copy in loads:
+        copy.start()
+    own.start()
 
     @pl.when(slab == 0)
     def _():
@@ -86,20 +120,35 @@
     def _():
         raw[:, HALO + slab_ch :] = jnp.full((rows, HALO), jnp.inf, F32)
 
-    load.wait()
-    own_rows = pl.multiple_of(g * rows, 8)
-    own = pltpu.make_async_copy(
-        held.at[pl.ds(own_rows, rows), :], raw.at[:, pl.ds(own_col, ch)], own_sem
-    )
-    own.start()
-    pl.semaphore_wait(barrier, n_chan - 1)
+    near = group - 1 + jnp.where(slab > 0, 1, 0) + jnp.where(slab < slabs - 1, 1, 0)
+    pl.semaphore_wait(barrier, near)
+
+    points = min(slabs, 3)
+
+    def relay(point):
+        for up in (True, False):
+            place = slab if up else slabs - 1 - slab
+            sem = token.at[0 if up else 1]
+            to = me + group if up else me - group
+            turn = (place == point) if point < points - 1 else (place >= point)
+
+            @pl.when(turn)
+            def _():
+                if point > 0:
+                    pl.semaphore_wait(sem, 1)
+
+                @pl.when(place < slabs - 1)
+                def _():
+                    pl.semaphore_signal(
+                        sem, inc=1, device_id={"chan": to}, device_id_type=MESH
+                    )
 
     def chunk(c):
-        return pl.ds(c * part, part)
+        return pl.ds(*spans[c])
 
     def slab_send(c, b):
         return pltpu.make_async_remote_copy(
-            src_ref=held.at[pl.ds(b * rows + c * part, part), :],
+            src_ref=cube.at[pl.ds(b * rows + spans[c][0], spans[c][1]), :],
             dst_ref=raw.at[chunk(c), pl.ds(own_col, ch)],
             send_sem=send_sem, recv_sem=recv_sem.at[c, g],
             device_id=peer(b), device_id_type=MESH,
@@ -107,7 +156,7 @@
 
     def slab_recv(c, b):
         return pltpu.make_async_remote_copy(
-            src_ref=held.at[pl.ds(c * part, part), :],
+            src_ref=cube.at[chunk(c), :],
             dst_ref=raw.at[chunk(c), pl.ds(HALO + b * ch, ch)],
             send_sem=send_sem, recv_sem=recv_sem.at[c, b],
             device_id=peer(b), device_id_type=MESH,
@@ -121,7 +170,7 @@
             col = HALO + slab_ch + b * ch
             sem, to = down_sem.at[c], me - group
         if from_own:
-            src = held.at[pl.ds(pl.multiple_of(own_rows + c * part, 8), part), :]
+            src = cube.at[pl.ds(pl.multiple_of(own_rows + spans[c][0], 8), spans[c][1]), :]
         else:
             src = raw.at[chunk(c), pl.ds(HALO + b * ch, ch)]
         return pltpu.make_async_remote_copy(
@@ -178,12 +227,15 @@
         def _():
             arrived(HALO + slab_ch, down_sem.at[c]).wait_recv()
 
-    for c in range(CHUNKS):
+    for c in range(len(spans)):
         for b in range(group):
             @pl.when(g != b)
             def _():
                 slab_send(c, b).start()
         own_hops(c)
+    relay(0)
+    for copy in loads:
+        copy.wait()
 
     shape = mask_sq.shape
     index = lax.broadcasted_iota(jnp.int32, shape, 0) * shape[1] + lax.broadcasted_iota(
@@ -228,17 +280,17 @@
     forward(1)
 
     own.wait()
-    lane = lax.broadcasted_iota(jnp.int32, (BLOCK, LANES), 1)
     edge = HALO // LANES
 
-    def snip(start):
-        r = pl.ds(start, BLOCK)
+    def snip(start, block):
+        r = pl.ds(start, block)
+        lane = lax.broadcasted_iota(jnp.int32, (block, LANES), 1)
 
         def at(ref, t):
-            return ref[:, (t + edge) * LANES : (t + edge + 1) * LANES]
+            return ref[0:block, (t + edge) * LANES : (t + edge + 1) * LANES]
 
         def put(ref, t, v):
-            ref[:, (t + edge) * LANES : (t + edge + 1) * LANES] = v
+            ref[0:block, (t + edge) * LANES : (t + edge + 1) * LANES] = v
 
         def first(t):
             return raw[r, (t + edge) * LANES : (t + edge + 1) * LANES]
@@ -271,30 +323,34 @@
                     put(dst, t, v)
                 else:
                     cols = slice(t * LANES, (t + 1) * LANES)
-                    hi = v.astype(BF16)
-                    fit_hi[r, cols] = hi
-                    fit_lo[r, cols] = (v - hi.astype(F32)).astype(BF16)
+                    fit[r, cols] = v
             src, dst = dst, src
 
     def process(c):
         halo_wait(c)
-        blocks = part // BLOCK
-        if blocks == 1:
-            snip(c * part)
+        first_row, part = spans[c]
+        block = min(BLOCK, part)
+        if part == block:
+            snip(first_row, block)
         else:
             def body(i, carry):
-                snip(pl.multiple_of(c * part + i * BLOCK, BLOCK))
+                snip(pl.multiple_of(first_row + i * block, 8), block)
                 return carry
-            lax.fori_loop(0, blocks, body, 0)
-
-    for c in range(CHUNKS):
-        if c + 2 < CHUNKS:
+            lax.fori_loop(0, part // block, body, 0)
+
+    for c in range(len(spans)):
+        if c + 2 < len(spans):
             forward(c + 2)
         process(c)
+        if c in (0, 1) and c + 1 < points:
+            relay(c + 1)
 
     dims = (((1,), (1,)), ((), ()))
-    rhs3 = lax.dot_general(w3[...], fit_hi[...], dims, preferred_element_type=F32)
-    rhs3 = rhs3 + lax.dot_general(w3[...], fit_lo[...], dims, preferred_element_type=F32)
+    whole = fit[...]
+    fit_hi = whole.astype(BF16)
+    fit_lo = (whole - fit_hi.astype(F32)).astype(BF16)
+    rhs3 = lax.dot_general(w3[...], fit_hi, dims, preferred_element_type=F32)
+    rhs3 = rhs3 + lax.dot_general(w3[...], fit_lo, dims, preferred_element_type=F32)
     rhs = rhs3[0:TERMS] + (rhs3[TERMS : 2 * TERMS] + rhs3[2 * TERMS :])
     fold = sums.shape[2] // rows
     high = TERMS // fold
@@ -317,7 +373,9 @@
         shaped = shaped + inverse[:, m : m + 1] * t_own[m : m + 1, :]
     a_hi, a_mid, a_lo = split3(shaped)
     zero = jnp.zeros_like(a_hi)
-    right_side = jnp.concatenate([a_hi, a_mid, a_hi, a_lo, a_hi, a_mid, zero, zero], axis=0)
+    right_out[...] = jnp.concatenate(
+        [a_hi, a_mid, a_hi, a_lo, a_hi, a_mid, zero, zero], axis=0
+    )
 
     def sent(ref, sem):
         return pltpu.make_async_remote_copy(
@@ -326,7 +384,7 @@
         )
 
     if group > 1:
-        sent(held.at[0 : (group - 1) * rows, :], send_sem).wait_send()
+        sent(cube.at[0 : (group - 1) * rows, :], send_sem).wait_send()
 
     @pl.when(slab < slabs - 1)
     def _():
@@ -354,9 +412,11 @@
         hi, mid, lo = (v.astype(F32) for v in split3(tot))
         none = jnp.zeros_like(hi)
         left_side = jnp.concatenate([hi, hi, mid, hi, lo, mid, none, none], axis=0)
-        left_side = left_side.T.astype(BF16)
-        r = slice(b * rows, (b + 1) * rows)
-        out[r, :] = held[r, :] - jnp.dot(left_side, right_side, preferred_element_type=F32)
+        left_out[b * rows : (b + 1) * rows, :] = left_side.T.astype(BF16)
+
+
+def subtract(cube, left, right, out):
+    out[...] = cube[...] - jnp.dot(left[...], right[...], preferred_element_type=F32)
 
 
 def per_device(cube, windows, mask):
@@ -369,35 +429,50 @@
     wide = slab_ch + 2 * HALO
     fold = max(1, LANES // rows)
     vmem = pl.BlockSpec(memory_space=pltpu.VMEM)
+    hbm = pl.BlockSpec(memory_space=pl.ANY)
     dma = pltpu.SemaphoreType.DMA
-    return pl.pallas_call(
+    chunks = len(chunk_spans(rows))
+    lin = jnp.asarray(linearization())
+    depth = 8 * TERMS
+    left, right = pl.pallas_call(
         functools.partial(kernel, n_chan, group, total),
-        out_shape=jax.ShapeDtypeStruct((pix, ch), F32),
-        in_specs=[
-            pl.BlockSpec(memory_space=pltpu.SMEM),
-            pl.BlockSpec(memory_space=pl.ANY),
-            vmem, vmem, vmem,
-        ],
-        out_specs=vmem,
+        out_shape=(
+            jax.ShapeDtypeStruct((pix, depth), BF16),
+            jax.ShapeDtypeStruct((depth, ch), BF16),
+        ),
+        in_specs=[pl.BlockSpec(memory_space=pltpu.SMEM), hbm, hbm, hbm, hbm],
+        out_specs=(vmem, vmem),
         scratch_shapes=[
-            pltpu.VMEM((pix, ch), F32),
+            pltpu.VMEM((total // LANES, LANES), jnp.int32),
+            pltpu.VMEM((1, total), jnp.int32),
+            pltpu.VMEM(lin.shape, F32),
             pltpu.VMEM((rows, wide), F32),
             pltpu.VMEM((BLOCK, wide), F32),
             pltpu.VMEM((BLOCK, wide), F32),
-            pltpu.VMEM((rows, slab_ch), BF16),
-            pltpu.VMEM((rows, slab_ch), BF16),
+            pltpu.VMEM((rows, slab_ch), F32),
             pltpu.VMEM((TERMS, slab_ch), F32),
             pltpu.VMEM((3 * TERMS, slab_ch), BF16),
             pltpu.VMEM((n_chan, TERMS // fold, rows * fold), F32),
-            dma, dma, dma, dma((2,)),
-            dma((CHUNKS, group)), dma((CHUNKS,)), dma((CHUNKS,)),
+            dma((3,)), pltpu.SemaphoreType.REGULAR((2,)), dma, dma, dma((2,)),
+            dma((chunks, group)), dma((chunks,)), dma((chunks,)),
             dma, dma,
         ],
-        compiler_params=pltpu.CompilerParams(collective_id=0, has_side_effects=True),
-    )(
-        windows, cube, mask.reshape(-1, LANES), mask.reshape(1, total),
-        jnp.asarray(linearization()),
-    )
+        compiler_params=pltpu.CompilerParams(
+            collective_id=0, has_side_effects=True
+        ),
+    )(windows, cube, mask.reshape(-1, LANES), mask.reshape(1, total), lin)
+    step = max(pix // SPLIT, 16)
+    return pl.pallas_call(
+        subtract,
+        grid=(pix // step,),
+        out_shape=jax.ShapeDtypeStruct((pix, ch), F32),
+        in_specs=[
+            pl.BlockSpec((step, ch), lambda i: (i, 0)),
+            pl.BlockSpec((step, depth), lambda i: (i, 0)),
+            pl.BlockSpec((depth, ch), lambda i: (0, 0)),
+        ],
+        out_specs=pl.BlockSpec((step, ch), lambda i: (i, 0)),
+    )(cube, left, right)
 
 
 def solution(mesh):

time: 33.1 us -> 31.5 us (0.952)
  local copies, waits for them, and re-layouts: 2.31 us -> 0 us
  Pallas kernels: 30.6 us -> 31.4 us
    pallas_call x0 -> x1, Pallas kernels: none -> 2.39 us  [per_device(): pl.pallas_call(subtract, grid=(pix // step,), out_shape=jax.ShapeDtypeStr...]
    unnamed x1 -> x0, local copies, waits for them, and re-layouts: 2.31 us -> none
    pallas_call x1, Pallas kernels: 30.6 us -> 29 us  [per_device(): pl.pallas_call(functools.partial(kernel, n_chan, group, total), out_shape...]
where the time goes in v2:
time: 31.5 us; the launch traced here: 31.4 us
  Pallas kernels  31.4 us (100%)
    pallas_call x1, Pallas kernels, per_device(): pl.pallas_call(functools.partial(kernel, n_chan, group, total), out_shape...  29 us
    pallas_call x1, Pallas kernels, per_device(): pl.pallas_call(subtract, grid=(pix // step,), out_shape=jax.ShapeDtypeStr...  2.39 us

profile of v2, /device:TPU:0, one launch (start us, length us, event | category | flops | bytes accessed | tf_op | source)
XLA Modules:
  0.0 31.4 jit_solution(14604535279575402581)
XLA Ops:
  0.0 29.0 %shard_map.46 = (bf16[256,128]{1,0:T(8,128)(2,1)}, bf16[128,1024]{1,0:T(8,128)(2,1)}) custom-call(s32[8]{0:T(128)} %windows.1, f32[256,1024]{1,0:T(8,128)} %cube.3, s32[128,128]{1,0:T(8,128)} %bitcast.2, s32[1,16384]{1,0:T(1,128)} %bitcast.3, f32[31,16,16]{2,1,0:T(8,128)} %constant.2.clone.lin_hbm), custom_call_target="tpu_custom_call" | custom-call | tf_op jit(solution)/shard_map/pallas_call | solution.py:437
  29.0 2.4 %shard_map.47 = f32[256,1024]{1,0:T(8,128)} custom-call(f32[256,1024]{1,0:T(8,128)} %cube.3, bf16[256,128]{1,0:T(8,128)(2,1)} %get-tuple-element.7.left, bf16[128,1024]{1,0:T(8,128)(2,1)} %get-tuple-element.8.right), custom_call_target="tpu_custom_call" | custom-call | tf_op jit(solution)/shard_map/pallas_call | solution.py:465

commit v3 on v2

--- a/solution.py
+++ b/solution.py
@@ -62,10 +62,10 @@
 
 def kernel(
     n_chan, group, total,
-    windows, cube, mask_sq_hbm, mask_row_hbm, lin_hbm,
-    left_out, right_out,
-    mask_sq, mask_row, lin, raw, ping, pong, fit, table, w3, sums,
-    load_sem, token, own_sem, send_sem, hop_sem, recv_sem, up_sem, down_sem, sum_send, sum_recv,
+    windows_hbm, cube, mask_sq_hbm, mask_row_hbm, lin_hbm,
+    left_out, right_hbm,
+    windows, right_out, mask_sq, mask_row, lin, raw, ping, pong, fit, table, w3, sums,
+    load_sem, right_sem, token, own_sem, send_sem, hop_sem, recv_sem, up_sem, down_sem, sum_send, sum_recv,
 ):
     pix, ch = cube.shape
     rows = raw.shape[0]
@@ -104,6 +104,7 @@
         pltpu.make_async_copy(mask_sq_hbm, mask_sq, load_sem.at[0]),
         pltpu.make_async_copy(mask_row_hbm, mask_row, load_sem.at[1]),
         pltpu.make_async_copy(lin_hbm, lin, load_sem.at[2]),
+        pltpu.make_async_copy(windows_hbm, windows, load_sem.at[3]),
     ]
     own = pltpu.make_async_copy(
         cube.at[pl.ds(own_rows, rows), :], raw.at[:, pl.ds(own_col, ch)], own_sem
@@ -338,20 +339,26 @@
                 return carry
             lax.fori_loop(0, part // block, body, 0)
 
+    dims = (((1,), (1,)), ((), ()))
+
+    def products(lo, hi):
+        whole = fit[lo:hi, :]
+        fit_hi = whole.astype(BF16)
+        fit_lo = (whole - fit_hi.astype(F32)).astype(BF16)
+        rhs3 = lax.dot_general(w3[...], fit_hi, dims, preferred_element_type=F32)
+        rhs3 = rhs3 + lax.dot_general(w3[...], fit_lo, dims, preferred_element_type=F32)
+        return rhs3[0:TERMS] + (rhs3[TERMS : 2 * TERMS] + rhs3[2 * TERMS :])
+
+    cut = rows * (CHUNKS - 1) // CHUNKS
     for c in range(len(spans)):
         if c + 2 < len(spans):
             forward(c + 2)
         process(c)
         if c in (0, 1) and c + 1 < points:
             relay(c + 1)
-
-    dims = (((1,), (1,)), ((), ()))
-    whole = fit[...]
-    fit_hi = whole.astype(BF16)
-    fit_lo = (whole - fit_hi.astype(F32)).astype(BF16)
-    rhs3 = lax.dot_general(w3[...], fit_hi, dims, preferred_element_type=F32)
-    rhs3 = rhs3 + lax.dot_general(w3[...], fit_lo, dims, preferred_element_type=F32)
-    rhs = rhs3[0:TERMS] + (rhs3[TERMS : 2 * TERMS] + rhs3[2 * TERMS :])
+        if sum(spans[c]) == cut:
+            early = products(0, cut)
+    rhs = jnp.concatenate([early, products(cut, rows)], axis=1)
     fold = sums.shape[2] // rows
     high = TERMS // fold
     packed = jnp.concatenate([rhs[i * high : (i + 1) * high] for i in range(fold)], axis=1)
@@ -376,6 +383,8 @@
     right_out[...] = jnp.concatenate(
         [a_hi, a_mid, a_hi, a_lo, a_hi, a_mid, zero, zero], axis=0
     )
+    right_copy = pltpu.make_async_copy(right_out, right_hbm, right_sem)
+    right_copy.start()
 
     def sent(ref, sem):
         return pltpu.make_async_remote_copy(
@@ -401,6 +410,7 @@
     )
     everyone.wait_send()
     everyone.wait_recv()
+    right_copy.wait()
 
     for b in range(group):
         tot = sums[b]
@@ -440,9 +450,11 @@
             jax.ShapeDtypeStruct((pix, depth), BF16),
             jax.ShapeDtypeStruct((depth, ch), BF16),
         ),
-        in_specs=[pl.BlockSpec(memory_space=pltpu.SMEM), hbm, hbm, hbm, hbm],
-        out_specs=(vmem, vmem),
+        in_specs=[hbm, hbm, hbm, hbm, hbm],
+        out_specs=(vmem, hbm),
         scratch_shapes=[
+            pltpu.SMEM(windows.shape, jnp.int32),
+            pltpu.VMEM((depth, ch), BF16),
             pltpu.VMEM((total // LANES, LANES), jnp.int32),
             pltpu.VMEM((1, total), jnp.int32),
             pltpu.VMEM(lin.shape, F32),
@@ -453,7 +465,7 @@
             pltpu.VMEM((TERMS, slab_ch), F32),
             pltpu.VMEM((3 * TERMS, slab_ch), BF16),
             pltpu.VMEM((n_chan, TERMS // fold, rows * fold), F32),
-            dma((3,)), pltpu.SemaphoreType.REGULAR((2,)), dma, dma, dma((2,)),
+            dma((4,)), dma, pltpu.SemaphoreType.REGULAR((2,)), dma, dma, dma((2,)),
             dma((chunks, group)), dma((chunks,)), dma((chunks,)),
             dma, dma,
         ],

time: 31.5 us -> 31.3 us (level)
  no operation moved by 1% of the time
where the time goes in v3:
time: 31.3 us; the launch traced here: 31.1 us
  Pallas kernels  31.1 us (99%)
    pallas_call x1, Pallas kernels, per_device(): pl.pallas_call(functools.partial(kernel, n_chan, group, total), out_shape...  28.7 us
    pallas_call x1, Pallas kernels, per_device(): pl.pallas_call(subtract, grid=(pix // step,), out_shape=jax.ShapeDtypeStr...  2.39 us

profile of v3, /device:TPU:0, one launch (start us, length us, event | category | flops | bytes accessed | tf_op | source)
XLA Modules:
  0.0 31.1 jit_solution(13932147351211788028)
XLA Ops:
  0.0 28.7 %shard_map.46 = (bf16[256,128]{1,0:T(8,128)(2,1)}, bf16[128,1024]{1,0:T(8,128)(2,1)}) custom-call(s32[8]{0:T(128)} %windows_hbm.1, f32[256,1024]{1,0:T(8,128)} %cube.3, s32[128,128]{1,0:T(8,128)} %bitcast.2, s32[1,16384]{1,0:T(1,128)} %bitcast.3, f32[31,16,16]{2,1,0:T(8,128)} %constant.2.clone.lin_hbm), custom_call_target="tpu_custom_call" | custom-call | tf_op jit(solution)/shard_map/pallas_call | solution.py:447
  28.7 2.4 %shard_map.47 = f32[256,1024]{1,0:T(8,128)} custom-call(f32[256,1024]{1,0:T(8,128)} %cube.3, bf16[256,128]{1,0:T(8,128)(2,1)} %get-tuple-element.7.left, bf16[128,1024]{1,0:T(8,128)(2,1)} %get-tuple-element.8.right), custom_call_target="tpu_custom_call" | custom-call | tf_op jit(solution)/shard_map/pallas_call | solution.py:477
